TPU v7x, 32 devices: a whole 2x2x4 slice. The times are simulated.
32 devices in a mesh: rep: 2 (over y), shard: 16 (over z, x, core).
Axes of the slice: x: 2, y: 2, z: 4, core: 2. Of those that a mesh axis runs over, the one named last changes fastest.
Arguments:
- block_input: bfloat16 [32768, 768], P(('rep', 'shard')), may hold values from -6 to 6
- history: bfloat16 [4, 32768, 768], P(None, ('rep', 'shard')), may hold values from -6 to 6
- cotangent: bfloat16 [32768, 768], P(('rep', 'shard')), may hold values from -6 to 6
- span_start: int32 [32], P(('rep', 'shard')), may hold values from 0 to 768, as said below
- w_qkv: bfloat16 [768, 2304], P('shard'), may hold values from -0.21875 to 0.21875
- w_out: bfloat16 [768, 768], P('shard'), may hold values from -4 to 4
- w_up: bfloat16 [768, 3072], P('shard'), may hold values from -0.21875 to 0.21875
- w_down: bfloat16 [3072, 768], P('shard'), may hold values from -0.109375 to 0.109375
- ln_gains: bfloat16 [2, 768], P(None, 'shard'), may hold values from 0.5 to 1.5
- ln_biases: bfloat16 [2, 768], P(None, 'shard'), may hold values from -3 to 3
- mix_weights: float32 [5], replicated, may hold values from 0.3 to 1
Outputs:
- next_input: bfloat16 [32768, 768], P(('rep', 'shard'))
- grad_input: float32 [32768, 768], P(('rep', 'shard'))
- grad_history: float32 [4, 32768, 768], P(None, ('rep', 'shard'))
- grad_mix: float32 [5], replicated
- grad_w_qkv: float32 [768, 2304], P('shard')
- grad_w_out: float32 [768, 768], P('shard')
- grad_w_up: float32 [768, 3072], P('shard')
- grad_w_down: float32 [3072, 768], P('shard')
- grad_gains: float32 [2, 768], P(None, 'shard')
- grad_bias_first: float32 [768], P('shard')
- grad_bias_second: float32 [768], P('shard')
Inputs may be any that keep to these rules, and one draw needn't show every extreme that they name: Sequence n's picture span covers positions span_start[n] to span_start[n] + 255 of that sequence.
All inputs are finite; a program needn't handle non-finite values.
Results may differ from a plain program's by a relative error of at most 0.017.
Values may be sent and summed in bfloat16 or wider, within the bound.
A program may use at most 256 MiB of HBM per device.

v0:
```python
import jax
import jax.numpy as jnp
from jax import lax
from jax.sharding import PartitionSpec as P

HEADS = 12
SPAN = 256
eps = 1e-05


def layer_norm(values, gain_row, bias_row):
    average = jnp.mean(values, axis=-1, keepdims=True)
    centered = values - average
    inverse_std = lax.rsqrt(jnp.mean(centered * centered, axis=-1, keepdims=True) + eps)
    normed = centered * inverse_std
    return (normed * gain_row + bias_row, normed, inverse_std)


def layer_norm_back(incoming, normed, inverse_std, gain_row):
    scaled = incoming * gain_row
    inner = (
        scaled
        - jnp.mean(scaled, axis=-1, keepdims=True)
        - normed * jnp.mean(scaled * normed, axis=-1, keepdims=True)
    )
    return (inverse_std * inner, jnp.sum(incoming * normed, axis=0), jnp.sum(incoming, axis=0))


def rotary_tables(length, head_width):
    half_width = head_width // 2
    frequency = jnp.exp(
        -jnp.log(10000.0) * jnp.arange(half_width, dtype=jnp.float32) * (2.0 / head_width)
    )
    angles = jnp.arange(length, dtype=jnp.float32)[:, None] * frequency[None, :]
    angles = jnp.concatenate([angles, angles], axis=-1)[:, None, :]
    return (jnp.cos(angles), jnp.sin(angles))


def rotate(values, cosine, sine):
    half_width = values.shape[-1] // 2
    turned = jnp.concatenate([-values[..., half_width:], values[..., :half_width]], axis=-1)
    return values * cosine + turned * sine


def rotate_back(incoming, cosine, sine):
    half_width = incoming.shape[-1] // 2
    weighted = incoming * sine
    turned = jnp.concatenate([weighted[..., half_width:], -weighted[..., :half_width]], axis=-1)
    return incoming * cosine + turned


def gelu_parts(upper):
    normal_cdf = 0.5 * (1.0 + lax.erf(upper * 0.7071067811865476))
    density = jnp.exp(-0.5 * upper * upper) * 0.3989422804014327
    return (upper * normal_cdf, normal_cdf + upper * density)


def visible(row_pos, col_pos, span_begin):
    row_in = (row_pos >= span_begin) & (row_pos < span_begin + SPAN)
    col_in = (col_pos >= span_begin) & (col_pos < span_begin + SPAN)
    return (col_pos[None, :] <= row_pos[:, None]) | row_in[:, None] & col_in[None, :]


def block_scores(query_block, key_rows, row_pos, col_pos, span_begin):
    factor = query_block.shape[2] ** (-0.5)
    scores = (
        jnp.einsum("qhd,khd->hqk", query_block, key_rows, preferred_element_type=jnp.float32)
        * factor
    )
    return jnp.where(visible(row_pos, col_pos, span_begin)[None], scores, -1e30)


def attend_forward(query_rows, key_rows, value_rows, span_begin):
    length = query_rows.shape[0]
    block_rows = min(512, length)
    block_count = length // block_rows
    col_pos = jnp.arange(length, dtype=jnp.int32)

    def one_block(block_index):
        first_row = block_index * block_rows
        row_pos = first_row + jnp.arange(block_rows, dtype=jnp.int32)
        query_block = lax.dynamic_slice_in_dim(query_rows, first_row, block_rows, 0)
        scores = block_scores(query_block, key_rows, row_pos, col_pos, span_begin)
        row_max = jnp.max(scores, axis=-1, keepdims=True)
        log_sums = row_max + jnp.log(jnp.sum(jnp.exp(scores - row_max), axis=-1, keepdims=True))
        attn_probs = jnp.exp(scores - log_sums).astype(jnp.bfloat16)
        block_out = jnp.einsum(
            "hqk,khd->qhd", attn_probs, value_rows, preferred_element_type=jnp.float32
        )
        return (block_out.astype(jnp.bfloat16), log_sums[..., 0])

    outputs, log_sums = lax.map(one_block, jnp.arange(block_count, dtype=jnp.int32))
    return (outputs.reshape(query_rows.shape), log_sums)


def attend_backward(query_rows, key_rows, value_rows, grad_rows, log_sums, span_begin):
    length = query_rows.shape[0]
    block_rows = min(512, length)
    block_count = length // block_rows
    col_pos = jnp.arange(length, dtype=jnp.int32)
    factor = query_rows.shape[2] ** (-0.5)

    def one_block(running, block_index):
        grad_keys, grad_values = running
        first_row = block_index * block_rows
        row_pos = first_row + jnp.arange(block_rows, dtype=jnp.int32)
        query_block = lax.dynamic_slice_in_dim(query_rows, first_row, block_rows, 0)
        grad_block = lax.dynamic_slice_in_dim(grad_rows, first_row, block_rows, 0)
        scores = block_scores(query_block, key_rows, row_pos, col_pos, span_begin)
        attn_probs = jnp.exp(scores - log_sums[block_index][..., None])
        grad_probs = jnp.einsum(
            "qhd,khd->hqk", grad_block, value_rows, preferred_element_type=jnp.float32
        )
        delta_sum = jnp.sum(attn_probs * grad_probs, axis=-1, keepdims=True)
        grad_scores = (attn_probs * (grad_probs - delta_sum)).astype(jnp.bfloat16)
        grad_query = (
            jnp.einsum("hqk,khd->qhd", grad_scores, key_rows, preferred_element_type=jnp.float32)
            * factor
        )
        grad_keys = (
            grad_keys
            + jnp.einsum(
                "hqk,qhd->khd", grad_scores, query_block, preferred_element_type=jnp.float32
            )
            * factor
        )
        grad_values = grad_values + jnp.einsum(
            "hqk,qhd->khd",
            attn_probs.astype(jnp.bfloat16),
            grad_block,
            preferred_element_type=jnp.float32,
        )
        return ((grad_keys, grad_values), grad_query)

    zero_rows = jnp.zeros(key_rows.shape, jnp.float32)
    (grad_keys, grad_values), grad_queries = lax.scan(
        one_block, (zero_rows, zero_rows), jnp.arange(block_count, dtype=jnp.int32)
    )
    return (grad_queries.reshape(query_rows.shape), grad_keys, grad_values)


def local(
    block_input,
    history,
    cotangent,
    span_start,
    w_qkv,
    w_out,
    w_up,
    w_down,
    ln_gains,
    ln_biases,
    mix_weights,
):
    tokens, model_width = block_input.shape
    seq_count = span_start.shape[0]
    length = tokens // seq_count
    head_count = HEADS
    head_width = model_width // head_count
    past_count = history.shape[0]
    full_qkv, full_out, full_up, full_down, gains_low, biases_low = (
        lax.all_gather(w_qkv, "shard", axis=0, tiled=True),
        lax.all_gather(w_out, "shard", axis=0, tiled=True),
        lax.all_gather(w_up, "shard", axis=0, tiled=True),
        lax.all_gather(w_down, "shard", axis=0, tiled=True),
        lax.all_gather(ln_gains, "shard", axis=1, tiled=True),
        lax.all_gather(ln_biases, "shard", axis=1, tiled=True),
    )
    gains = gains_low.astype(jnp.float32)
    biases = biases_low.astype(jnp.float32)
    inputs_f = block_input.astype(jnp.float32)
    normed1_out, normed1, inverse1 = layer_norm(inputs_f, gains[0], biases[0])
    act1 = normed1_out.astype(jnp.bfloat16)
    projected = jnp.dot(act1, full_qkv, preferred_element_type=jnp.float32)
    cosine, sine = rotary_tables(length, head_width)
    split_shape = (seq_count, length, head_count, head_width)
    q_rot = rotate(projected[:, :model_width].reshape(split_shape), cosine, sine).astype(
        jnp.bfloat16
    )
    k_rot = rotate(
        projected[:, model_width : 2 * model_width].reshape(split_shape), cosine, sine
    ).astype(jnp.bfloat16)
    v_low = projected[:, 2 * model_width :].reshape(split_shape).astype(jnp.bfloat16)

    def forward_sequence(inputs_now):
        query_rows, key_rows, value_rows, span_begin = inputs_now
        return attend_forward(query_rows, key_rows, value_rows, span_begin)

    mixed, log_sums = lax.map(forward_sequence, (q_rot, k_rot, v_low, span_start))
    mixed = mixed.reshape(tokens, model_width)
    middle = inputs_f + jnp.dot(mixed, full_out, preferred_element_type=jnp.float32)
    normed2_out, normed2, inverse2 = layer_norm(middle, gains[1], biases[1])
    act2 = normed2_out.astype(jnp.bfloat16)
    upper = jnp.dot(act2, full_up, preferred_element_type=jnp.float32)
    activated, slope = gelu_parts(upper)
    hidden = activated.astype(jnp.bfloat16)
    output = middle + jnp.dot(hidden, full_down, preferred_element_type=jnp.float32)
    earlier = jnp.einsum("k,ktd->td", mix_weights[:past_count], history.astype(jnp.float32))
    next_input = (earlier + mix_weights[past_count] * output).astype(jnp.bfloat16)
    grad_f = cotangent.astype(jnp.float32)
    grad_history = mix_weights[:past_count][:, None, None] * grad_f[None]
    history_terms = jnp.einsum("ktd,td->k", history, cotangent, preferred_element_type=jnp.float32)
    partial_mix = jnp.concatenate([history_terms, jnp.sum(grad_f * output)[None]])
    grad_mix = lax.psum(partial_mix, ("rep", "shard"))
    full_qkv, full_out, full_up, full_down = (
        lax.all_gather(w_qkv, "shard", axis=0, tiled=True),
        lax.all_gather(w_out, "shard", axis=0, tiled=True),
        lax.all_gather(w_up, "shard", axis=0, tiled=True),
        lax.all_gather(w_down, "shard", axis=0, tiled=True),
    )
    grad_output = mix_weights[past_count] * grad_f
    grad_branch = grad_output.astype(jnp.bfloat16)
    grad_w_down = jnp.einsum("tf,td->fd", hidden, grad_branch, preferred_element_type=jnp.float32)
    grad_hidden = jnp.einsum(
        "td,fd->tf", grad_branch, full_down, preferred_element_type=jnp.float32
    )
    grad_upper = (grad_hidden * slope).astype(jnp.bfloat16)
    grad_w_up = jnp.einsum("td,tf->df", act2, grad_upper, preferred_element_type=jnp.float32)
    grad_act2 = jnp.einsum("tf,df->td", grad_upper, full_up, preferred_element_type=jnp.float32)
    grad_norm2, grad_gain2, grad_bias2 = layer_norm_back(grad_act2, normed2, inverse2, gains[1])
    grad_middle = grad_output + grad_norm2
    grad_attended = grad_middle.astype(jnp.bfloat16)
    grad_w_out = jnp.einsum("ti,tj->ij", mixed, grad_attended, preferred_element_type=jnp.float32)
    grad_mixed = jnp.einsum(
        "tj,ij->ti", grad_attended, full_out, preferred_element_type=jnp.float32
    ).astype(jnp.bfloat16)

    def backward_sequence(inputs_now):
        query_rows, key_rows, value_rows, grad_rows, sums_now, span_begin = inputs_now
        return attend_backward(query_rows, key_rows, value_rows, grad_rows, sums_now, span_begin)

    grad_q, grad_k, grad_v = lax.map(
        backward_sequence,
        (q_rot, k_rot, v_low, grad_mixed.reshape(split_shape), log_sums, span_start),
    )
    grad_q = rotate_back(grad_q, cosine, sine).reshape(tokens, model_width)
    grad_k = rotate_back(grad_k, cosine, sine).reshape(tokens, model_width)
    grad_projected = jnp.concatenate(
        [grad_q, grad_k, grad_v.reshape(tokens, model_width)], axis=1
    ).astype(jnp.bfloat16)
    grad_w_qkv = jnp.einsum("ti,tj->ij", act1, grad_projected, preferred_element_type=jnp.float32)
    grad_act1 = jnp.einsum(
        "tj,ij->ti", grad_projected, full_qkv, preferred_element_type=jnp.float32
    )
    grad_norm1, grad_gain1, grad_bias1 = layer_norm_back(grad_act1, normed1, inverse1, gains[0])
    grad_input = grad_middle + grad_norm1
    grad_gains = jnp.stack([grad_gain1, grad_gain2])
    grad_biases = jnp.stack([grad_bias1, grad_bias2])
    local_grads = (grad_w_qkv, grad_w_out, grad_w_up, grad_w_down, grad_gains, grad_biases)
    owned = (
        lax.psum_scatter(
            local_grads[0].astype(jnp.bfloat16), "shard", scatter_dimension=0, tiled=True
        ).astype(jnp.float32),
        lax.psum_scatter(
            local_grads[1].astype(jnp.bfloat16), "shard", scatter_dimension=0, tiled=True
        ).astype(jnp.float32),
        lax.psum_scatter(
            local_grads[2].astype(jnp.bfloat16), "shard", scatter_dimension=0, tiled=True
        ).astype(jnp.float32),
        lax.psum_scatter(
            local_grads[3].astype(jnp.bfloat16), "shard", scatter_dimension=0, tiled=True
        ).astype(jnp.float32),
        lax.psum_scatter(
            local_grads[4].astype(jnp.bfloat16), "shard", scatter_dimension=1, tiled=True
        ).astype(jnp.float32),
        lax.psum_scatter(
            local_grads[5].astype(jnp.bfloat16), "shard", scatter_dimension=1, tiled=True
        ).astype(jnp.float32),
    )
    owned = (
        lax.psum(owned[0].astype(jnp.bfloat16), "rep").astype(jnp.float32),
        lax.psum(owned[1].astype(jnp.bfloat16), "rep").astype(jnp.float32),
        lax.psum(owned[2].astype(jnp.bfloat16), "rep").astype(jnp.float32),
        lax.psum(owned[3].astype(jnp.bfloat16), "rep").astype(jnp.float32),
        lax.psum(owned[4].astype(jnp.bfloat16), "rep").astype(jnp.float32),
        lax.psum(owned[5].astype(jnp.bfloat16), "rep").astype(jnp.float32),
    )
    return (
        next_input,
        grad_input,
        grad_history,
        grad_mix,
        owned[0],
        owned[1],
        owned[2],
        owned[3],
        owned[4],
        owned[5][0],
        owned[5][1],
    )


def solution(mesh):
    placed = (
        P(("rep", "shard"), None),
        P(None, ("rep", "shard"), None),
        P(("rep", "shard"), None),
        P(("rep", "shard")),
        P("shard", None),
        P("shard", None),
        P("shard", None),
        P("shard", None),
        P(None, "shard"),
        P(None, "shard"),
        P(),
    )
    return jax.shard_map(
        local,
        mesh=mesh,
        in_specs=placed,
        out_specs=(
            P(("rep", "shard"), None),
            P(("rep", "shard"), None),
            P(None, ("rep", "shard"), None),
            P(),
            P("shard", None),
            P("shard", None),
            P("shard", None),
            P("shard", None),
            P(None, "shard"),
            P("shard"),
            P("shard"),
        ),
        check_vma=False,
    )
```

profile of v0, /device:TPU:0, one launch (start us, length us, event | category | flops | bytes accessed | tf_op | source)
XLA Modules:
  0.0 911.4 jit_solution(13864573590740779968)
XLA Ops:
  12.0 23.4 %all-gather = bf16[16,48,2]{1,2,0:T(2,128)(2,1)S(1)} all-gather(bf16[1,48,2]{1,2,0:T(2,128)(2,1)} %bitcast.170), channel_id=1, replica_groups=mesh['rep'=2,'shard'=16] {'shard'}, dimensions={0}, use_global_device_ids=true | all-gather | bytes 3264 | tf_op jit(solution)/shard_map/all_gather | solution.py:166
  35.5 17.7 %all-gather.1 = bf16[16,48,2]{1,2,0:T(2,128)(2,1)S(1)} all-gather(bf16[1,48,2]{1,2,0:T(2,128)(2,1)} %bitcast.171), channel_id=1, replica_groups=mesh['rep'=2,'shard'=16] {'shard'}, dimensions={0}, use_global_device_ids=true | all-gather | bytes 3264 | tf_op jit(solution)/shard_map/all_gather | solution.py:167
  55.0 1.8 copy.80
  59.3 9.4 %fusion.43 = f32[1,1024,768]{2,0,1:T(1,128)} fusion(bf16[4,1024,768]{2,1,0:T(8,128)(2,1)} %param.16, f32[5]{0:T(128)S(1)} %copy-done.50), kind=kOutput, calls=%fused_computation.65 | convolution fusion | flops 6291456 | bytes 9437204 | tf_op jit(solution)/shard_map/k,ktd->td/dot_general | solution.py:198
  68.7 8.5 copy.101
  77.8 6.3 fusion.79
  85.5 3.1 fusion.82
  88.6 2.6 copy.85
  91.2 3.7 copy.87
  94.9 3.5 copy.83
  98.4 2.3 fusion.69
  102.6 4.3 fusion.62
  106.9 78.3 %while.52 = (s32[]{:T(128)}, bf16[2,512,12,64]{1,3,2,0:T(8,128)(2,1)S(1)}, f32[2,12,512]{2,1,0:T(8,128)S(1)}, s32[2]{0:T(128)S(1)}, s32[]{:T(128)}, /*index=5*/s...) while((s32[]{:T(128)}, ...), condition=%wide.region_5.6_spmd.clone.clone, body=%wide.region_2.5_spmd.clone.clone.sunk | while | flops 1681784320 | bytes 82558176 | solution.py:92
  109.9 12.0 %fusion.130 = (f32[12,512]{1,0:T(8,128)S(1)}, f32[12,512,1024]{2,1,0:T(8,128)}) fusion(pred[512,1024]{1,0:T(8,128)(4,1)S(1)} %fusion.129, bf16[1024,12,64]{0,2,1:T(8,128)(2,1)S(1)} %get-tuple-element.733, bf16[1024,12,64]{0,2,1:T(8,128)(2,1)} %get-tuple-element.732, s32[]{:T(128)S(6)} %select_n.68), kind=kOutput, calls=%fused_computation.5.clone.1 | convolution fusion | flops 824174592 | bytes 28073988 | tf_op jit(solution)/shard_map/while/body/eval_jaxpr/while/body/eval_jaxpr/qhd,khd->hqk/dot_general | solution.py:67
  122.0 12.3 %exponential_reduce_fusion.2 = f32[12,512]{1,0:T(8,128)S(1)} fusion(f32[12,512,1024]{2,1,0:T(8,128)} %get-tuple-element.682, f32[12,512]{1,0:T(8,128)S(1)} %get-tuple-element.683, pred[512,1024]{1,0:T(8,128)(4,1)S(1)} %fusion.129), kind=kLoop, calls=%fused_computation.3.clone.1 | loop fusion | flops 25159680 | bytes 25739264 | tf_op jit(solution)/shard_map/while/body/eval_jaxpr/while/body/eval_jaxpr/reduce_sum | solution.py:85
  134.3 11.7 %fusion.131 = bf16[2,512,12,64]{1,3,2,0:T(8,128)(2,1)S(1)} fusion(bf16[2,512,12,64]{1,3,2,0:T(8,128)(2,1)S(1)} %get-tuple-element.714, s32[]{:T(128)S(6)} %copy.143, bf16[1024,12,64]{0,2,1:T(8,128)(2,1)} %get-tuple-element.734, f32[12,512,1024]{2,1,0:T(8,128)} %get-tuple-element.682, f32[12,512]{1,0:T(8,128)S(1)} %get-tuple-element.684, ...), kind=kOutput, calls=%fused_computation.12.clone.1 | convolution fusion | flops 830865408 | bytes 28082180 | tf_op jit(solution)/shard_map/while/body/eval_jaxpr/while/body/eval_jaxpr/hqk,khd->qhd/dot_general | solution.py:87
  149.1 12.0 %fusion.130 = (f32[12,512]{1,0:T(8,128)S(1)}, f32[12,512,1024]{2,1,0:T(8,128)}) fusion(pred[512,1024]{1,0:T(8,128)(4,1)S(1)} %fusion.129, bf16[1024,12,64]{0,2,1:T(8,128)(2,1)S(1)} %get-tuple-element.733, bf16[1024,12,64]{0,2,1:T(8,128)(2,1)} %get-tuple-element.732, s32[]{:T(128)S(6)} %select_n.68), kind=kOutput, calls=%fused_computation.5.clone.1 | convolution fusion | flops 824174592 | bytes 28073988 | tf_op jit(solution)/shard_map/while/body/eval_jaxpr/while/body/eval_jaxpr/qhd,khd->hqk/dot_general | solution.py:67
  161.1 12.0 %exponential_reduce_fusion.2 = f32[12,512]{1,0:T(8,128)S(1)} fusion(f32[12,512,1024]{2,1,0:T(8,128)} %get-tuple-element.682, f32[12,512]{1,0:T(8,128)S(1)} %get-tuple-element.683, pred[512,1024]{1,0:T(8,128)(4,1)S(1)} %fusion.129), kind=kLoop, calls=%fused_computation.3.clone.1 | loop fusion | flops 25159680 | bytes 25739264 | tf_op jit(solution)/shard_map/while/body/eval_jaxpr/while/body/eval_jaxpr/reduce_sum | solution.py:85
  173.2 11.6 %fusion.131 = bf16[2,512,12,64]{1,3,2,0:T(8,128)(2,1)S(1)} fusion(bf16[2,512,12,64]{1,3,2,0:T(8,128)(2,1)S(1)} %get-tuple-element.714, s32[]{:T(128)S(6)} %copy.143, bf16[1024,12,64]{0,2,1:T(8,128)(2,1)} %get-tuple-element.734, f32[12,512,1024]{2,1,0:T(8,128)} %get-tuple-element.682, f32[12,512]{1,0:T(8,128)S(1)} %get-tuple-element.684, ...), kind=kOutput, calls=%fused_computation.12.clone.1 | convolution fusion | flops 830865408 | bytes 28082180 | tf_op jit(solution)/shard_map/while/body/eval_jaxpr/while/body/eval_jaxpr/hqk,khd->qhd/dot_general | solution.py:87
  186.4 3.2 copy.88
  191.1 3.3 fusion.84
  196.5 13.6 %multiply_convert_fusion.1 = (bf16[1024,3072]{1,0:T(8,128)(2,1)}, f32[1024,3072]{1,0:T(8,128)}) fusion(bf16[768,3072]{1,0:T(8,128)(2,1)} %all-gather.11.cloned.1.call-done, f32[1024,768]{0,1:T(8,128)} %copy-done.8, f32[768]{0:T(1024)S(1)} %copy-done.45, f32[768]{0:T(1024)S(1)} %copy-done.40, f32[1024]{0:T(1024)S(1)} %add_rsqrt_fusion, ...), kind=kOutput, calls=%fused_computation.62 | convolution fusion | flops 4851499008 | bytes 26753024 | tf_op jit(solution)/shard_map/dot_general | solution.py:194
  210.1 12.8 %fusion.42 = bf16[1024,3072]{1,0:T(8,128)(2,1)S(1)} fusion(f32[1024,3072]{1,0:T(8,128)} %get-tuple-element.553, bf16[3072,768]{1,0:T(8,128)(2,1)} %all-gather.13.cloned.1.call-done, bf16[1024,768]{0,1:T(8,128)(2,1)S(1)} %copy-done.16, f32[]{:T(128)} %bitcast.4), kind=kOutput, calls=%fused_computation.60 | convolution fusion | flops 4865654784 | bytes 25165828 | tf_op jit(solution)/shard_map/td,fd->tf/dot_general | solution.py:214
  222.9 7.3 fusion.85
  230.3 3.5 copy.91
  233.8 4.6 multiply_reduce_fusion.2
  238.5 12.5 %multiply_reduce_fusion.3 = (f32[]{:T(128)}, bf16[1024,768]{0,1:T(8,128)(2,1)}, f32[1024,768]{0,1:T(8,128)S(1)}) fusion(bf16[1024,768]{0,1:T(8,128)(2,1)S(1)} %copy-done.16, f32[]{:T(128)} %bitcast.4, f32[1,1024,768]{1,2,0:T(8,128)} %copy.101, f32[1024]{0:T(1024)S(1)} %broadcast_multiply_fusion.4, f32[1024,768]{0,1:T(8,128)S(1)} %copy-done.9, ...), kind=kOutput, calls=%fused_computation.104 | convolution fusion | flops 4844421120 | bytes 26758152 | tf_op jit(solution)/shard_map/dot_general | solution.py:197
  252.7 3.9 convolution_convert_fusion.4
  256.7 4.4 convolution_convert_fusion.3
  261.1 239.0 %while.53 = (s32[]{:T(128)}, f32[1024,12,64]{0,2,1:T(8,128)}, f32[1024,12,64]{0,2,1:T(8,128)}, f32[2,512,12,64]{1,0,3,2:T(2,128)}, s32[2]{0:T(128)S(1)}, /*index...) while((s32[]{:T(128)}, f32[1024,12,64]{0,2,1:T(8,128)}, ...), condition=%wide.region_12.13_spmd.clone.clone, body=%wide.region_10.12_spmd.clone.clone.sunk | while | flops 4126801408 | bytes 231923056 | solution.py:136
  266.6 11.6 %fusion.141 = f32[12,512,1024]{2,1,0:T(8,128)} fusion(bf16[1024,12,64]{0,2,1:T(8,128)(2,1)S(1)} %get-tuple-element.781, bf16[1024,12,64]{0,2,1:T(8,128)(2,1)} %get-tuple-element.778, s32[]{:T(128)S(6)} %select_n.72), kind=kOutput, calls=%fused_computation.40.clone.1 | convolution fusion | flops 805306368 | bytes 27525124 | tf_op jit(solution)/shard_map/while/body/eval_jaxpr/while/body/eval_jaxpr/qhd,khd->hqk/dot_general | solution.py:67
  278.2 13.5 %bitcast_add_fusion.7 = f32[1024,12,64]{0,2,1:T(8,128)} fusion(f32[1024,12,64]{0,2,1:T(8,128)} %get-tuple-element.758, f32[12,512,1024]{2,1,0:T(8,128)} %fusion.141, f32[12,512]{1,0:T(8,128)S(1)} %dynamic-slice_bitcast_fusion.2, pred[512,1024]{1,0:T(8,128)(4,1)S(1)} %fusion.143, pred[]{:T(512)S(6)} %compare.3, ...), kind=kOutput, calls=%fused_computation.31.clone.1 | convolution fusion | flops 832045056 | bytes 32800772 | tf_op jit(solution)/shard_map/while/body/eval_jaxpr/while/body/eval_jaxpr/hqk,qhd->khd/dot_general | solution.py:127
  291.7 18.2 %multiply_reduce_fusion.9 = (f32[12,512]{1,0:T(8,128)S(1)}, f32[12,512,1024]{2,1,0:T(8,128)}) fusion(f32[12,512,1024]{2,1,0:T(8,128)} %fusion.141, f32[12,512]{1,0:T(8,128)S(1)} %dynamic-slice_bitcast_fusion.2, pred[512,1024]{1,0:T(8,128)(4,1)S(1)} %fusion.143, bf16[1024,12,64]{0,2,1:T(8,128)(2,1)} %get-tuple-element.784, ...), kind=kOutput, calls=%fused_computation.26.clone.1 | convolution fusion | flops 836757504 | bytes 53264388 | tf_op jit(solution)/shard_map/while/body/eval_jaxpr/while/body/eval_jaxpr/qhd,khd->hqk/dot_general | solution.py:111
  309.9 21.3 %multiply_convert_fusion.6 = bf16[12,512,1024]{2,1,0:T(8,128)(2,1)} fusion(f32[12,512,1024]{2,1,0:T(8,128)} %get-tuple-element.698, f32[12,512,1024]{2,1,0:T(8,128)} %fusion.141, f32[12,512]{1,0:T(8,128)S(1)} %get-tuple-element.699, f32[12,512]{1,0:T(8,128)S(1)} %dynamic-slice_bitcast_fusion.2, pred[512,1024]{1,0:T(8,128)(4,1)S(1)} %fusion.143), kind=kLoop, calls=%fused_computation.25.clone.1 | loop fusion | flops 37748736 | bytes 63488000 | tf_op jit(solution)/shard_map/while/body/eval_jaxpr/while/body/eval_jaxpr/convert_element_type | solution.py:115
  331.1 9.7 %multiply_bitcast_fusion.3 = f32[1,512,12,64]{1,3,2,0:T(8,128)} fusion(bf16[12,512,1024]{2,1,0:T(8,128)(2,1)} %multiply_convert_fusion.6, bf16[1024,12,64]{0,2,1:T(8,128)(2,1)S(1)} %get-tuple-element.781), kind=kOutput, calls=%fused_computation.35.clone.1 | convolution fusion | flops 805699584 | bytes 15728640 | tf_op jit(solution)/shard_map/while/body/eval_jaxpr/while/body/eval_jaxpr/hqk,khd->qhd/dot_general | solution.py:117
  340.8 9.0 bitcast_add_fusion.6
  351.4 28.7 %dynamic_update_slice.41 = f32[2,512,12,64]{1,0,3,2:T(2,128)} dynamic-update-slice(f32[2,512,12,64]{1,0,3,2:T(2,128)} %get-tuple-element.759, f32[1,512,12,64]{1,0,3,2:T(1,128)S(1)} %copy.136, s32[]{:T(128)S(6)} %copy.153, s32[]{:T(128)} %constant.129.clone.1..sunk.1, s32[]{:T(128)} %constant.129.clone.1..sunk.1, s32[]{:T(128)} %constant.129.clone.1..sunk.1) | dynamic-update-slice | bytes 3145732 | tf_op jit(solution)/shard_map/while/body/eval_jaxpr/while/body/jit(dynamic_update_index_in_dim)/dynamic_update_slice | solution.py:136
  385.1 11.5 %fusion.141 = f32[12,512,1024]{2,1,0:T(8,128)} fusion(bf16[1024,12,64]{0,2,1:T(8,128)(2,1)S(1)} %get-tuple-element.781, bf16[1024,12,64]{0,2,1:T(8,128)(2,1)} %get-tuple-element.778, s32[]{:T(128)S(6)} %select_n.72), kind=kOutput, calls=%fused_computation.40.clone.1 | convolution fusion | flops 805306368 | bytes 27525124 | tf_op jit(solution)/shard_map/while/body/eval_jaxpr/while/body/eval_jaxpr/qhd,khd->hqk/dot_general | solution.py:67
  396.6 14.2 %bitcast_add_fusion.7 = f32[1024,12,64]{0,2,1:T(8,128)} fusion(f32[1024,12,64]{0,2,1:T(8,128)} %get-tuple-element.758, f32[12,512,1024]{2,1,0:T(8,128)} %fusion.141, f32[12,512]{1,0:T(8,128)S(1)} %dynamic-slice_bitcast_fusion.2, pred[512,1024]{1,0:T(8,128)(4,1)S(1)} %fusion.143, pred[]{:T(512)S(6)} %compare.3, ...), kind=kOutput, calls=%fused_computation.31.clone.1 | convolution fusion | flops 832045056 | bytes 32800772 | tf_op jit(solution)/shard_map/while/body/eval_jaxpr/while/body/eval_jaxpr/hqk,qhd->khd/dot_general | solution.py:127
  410.8 18.1 %multiply_reduce_fusion.9 = (f32[12,512]{1,0:T(8,128)S(1)}, f32[12,512,1024]{2,1,0:T(8,128)}) fusion(f32[12,512,1024]{2,1,0:T(8,128)} %fusion.141, f32[12,512]{1,0:T(8,128)S(1)} %dynamic-slice_bitcast_fusion.2, pred[512,1024]{1,0:T(8,128)(4,1)S(1)} %fusion.143, bf16[1024,12,64]{0,2,1:T(8,128)(2,1)} %get-tuple-element.784, ...), kind=kOutput, calls=%fused_computation.26.clone.1 | convolution fusion | flops 836757504 | bytes 53264388 | tf_op jit(solution)/shard_map/while/body/eval_jaxpr/while/body/eval_jaxpr/qhd,khd->hqk/dot_general | solution.py:111
  428.9 21.2 %multiply_convert_fusion.6 = bf16[12,512,1024]{2,1,0:T(8,128)(2,1)} fusion(f32[12,512,1024]{2,1,0:T(8,128)} %get-tuple-element.698, f32[12,512,1024]{2,1,0:T(8,128)} %fusion.141, f32[12,512]{1,0:T(8,128)S(1)} %get-tuple-element.699, f32[12,512]{1,0:T(8,128)S(1)} %dynamic-slice_bitcast_fusion.2, pred[512,1024]{1,0:T(8,128)(4,1)S(1)} %fusion.143), kind=kLoop, calls=%fused_computation.25.clone.1 | loop fusion | flops 37748736 | bytes 63488000 | tf_op jit(solution)/shard_map/while/body/eval_jaxpr/while/body/eval_jaxpr/convert_element_type | solution.py:115
  450.2 9.7 %multiply_bitcast_fusion.3 = f32[1,512,12,64]{1,3,2,0:T(8,128)} fusion(bf16[12,512,1024]{2,1,0:T(8,128)(2,1)} %multiply_convert_fusion.6, bf16[1024,12,64]{0,2,1:T(8,128)(2,1)S(1)} %get-tuple-element.781), kind=kOutput, calls=%fused_computation.35.clone.1 | convolution fusion | flops 805699584 | bytes 15728640 | tf_op jit(solution)/shard_map/while/body/eval_jaxpr/while/body/eval_jaxpr/hqk,khd->qhd/dot_general | solution.py:117
  459.8 9.9 %bitcast_add_fusion.6 = f32[1024,12,64]{0,2,1:T(8,128)} fusion(f32[1024,12,64]{0,2,1:T(8,128)} %get-tuple-element.757, bf16[12,512,1024]{2,1,0:T(8,128)(2,1)} %multiply_convert_fusion.6, pred[]{:T(512)S(6)} %compare.3, bf16[1024,12,64]{0,2,1:T(8,128)(2,1)} %get-tuple-element.778, s32[]{:T(128)S(6)} %select_n.72), kind=kOutput, calls=%fused_computation.32.clone.1 | convolution fusion | flops 807665664 | bytes 19660804 | tf_op jit(solution)/shard_map/while/body/eval_jaxpr/while/body/eval_jaxpr/hqk,qhd->khd/dot_general | solution.py:122
  471.3 28.7 %dynamic_update_slice.41 = f32[2,512,12,64]{1,0,3,2:T(2,128)} dynamic-update-slice(f32[2,512,12,64]{1,0,3,2:T(2,128)} %get-tuple-element.759, f32[1,512,12,64]{1,0,3,2:T(1,128)S(1)} %copy.136, s32[]{:T(128)S(6)} %copy.153, s32[]{:T(128)} %constant.129.clone.1..sunk.1, s32[]{:T(128)} %constant.129.clone.1..sunk.1, s32[]{:T(128)} %constant.129.clone.1..sunk.1) | dynamic-update-slice | bytes 3145732 | tf_op jit(solution)/shard_map/while/body/eval_jaxpr/while/body/jit(dynamic_update_index_in_dim)/dynamic_update_slice | solution.py:136
  500.2 3.4 convert.33
  503.6 3.7 broadcast_in_dim.95
  516.8 6.0 convolution_convert_fusion.2
  523.5 9.8 %convolution_convert_fusion.1 = bf16[768,3072]{1,0:T(8,128)(2,1)} fusion(bf16[1024,3072]{1,0:T(8,128)(2,1)} %copy-done.55, f32[1024,768]{0,1:T(8,128)} %copy-done.8, f32[768]{0:T(1024)S(1)} %copy-done.46, f32[768]{0:T(1024)S(1)} %copy-done.41, f32[1024]{0:T(1024)S(1)} %copy-done.43, f32[1024]{0:T(1024)S(1)} %copy-done.39), kind=kOutput, calls=%fused_computation.68 | convolution fusion | flops 4838129664 | bytes 14170112 | tf_op jit(solution)/shard_map/td,tf->df/dot_general | solution.py:218
  534.7 10.9 %convolution_convert_fusion = bf16[3072,768]{1,0:T(8,128)(2,1)} fusion(bf16[1024,3072]{1,0:T(8,128)(2,1)} %get-tuple-element.552, bf16[1024,768]{0,1:T(8,128)(2,1)S(1)} %copy-done.17, f32[]{:T(128)} %bitcast.4), kind=kOutput, calls=%fused_computation.67 | convolution fusion | flops 4836556800 | bytes 12582916 | tf_op jit(solution)/shard_map/tf,td->fd/dot_general | solution.py:213
  545.7 3.2 copy.95
  549.2 5.3 multiply_reduce_fusion.1
  554.5 6.9 broadcast_multiply_fusion
  561.4 5.6 fusion.86
  567.9 3.5 copy.94
  571.4 3.1 fusion.57
  576.2 38.4 %psum.49 = f32[5]{0:T(128)} all-reduce(f32[5]{0:T(128)S(1)} %pad_maximum_fusion.7), channel_id=1, replica_groups=mesh['rep'=2,'shard'=16] {'rep','shard'}, use_global_device_ids=true, to_apply=%region_16.17 | all-reduce | flops 5 | bytes 40 | tf_op jit(solution)/shard_map/psum | solution.py:204
  616.2 51.8 %reduce-scatter.15.cloned.1.call-done = bf16[48,3072]{1,0:T(8,128)(2,1)} async-done(((bf16[768,3072]{1,0:T(8,128)(2,1)}), bf16[48,3072]{1,0:T(8,128)(2,1)}) %reduce-scatter.15.cloned.1.call-update) | async-done | bytes 294928 | tf_op jit(solution)/shard_map/reduce_scatter | solution.py:257
  667.9 78.5 %reduce-scatter.17.cloned.1.call-done = bf16[192,768]{1,0:T(8,128)(2,1)} async-done(((bf16[3072,768]{1,0:T(8,128)(2,1)}), bf16[192,768]{1,0:T(8,128)(2,1)}) %reduce-scatter.17.cloned.1.call-update) | async-done | bytes 294928 | tf_op jit(solution)/shard_map/reduce_scatter | solution.py:260
  746.5 5.4 fusion.56
  752.0 3.5 copy.99
  755.5 47.6 %reduce-scatter.21.cloned.1.call-done = bf16[48,2]{1,0:T(8,128)(2,1)} async-done(((bf16[768,2]{1,0:T(8,128)(2,1)}), bf16[48,2]{1,0:T(8,128)(2,1)}) %reduce-scatter.21.cloned.1.call-update) | async-done | bytes 208
  803.9 55.5 %reduce-scatter.19.cloned.1.call-done = bf16[48,2]{1,0:T(8,128)(2,1)} async-done(((bf16[768,2]{1,0:T(8,128)(2,1)}), bf16[48,2]{1,0:T(8,128)(2,1)}) %reduce-scatter.19.cloned.1.call-update) | async-done | bytes 208
  860.2 4.9 all-reduce
  866.2 31.3 %all-reduce.4.cloned.1.call-done = (bf16[48,2304]{1,0:T(8,128)(2,1)}, bf16[48,768]{1,0:T(8,128)(2,1)}, bf16[48,3072]{1,0:T(8,128)(2,1)}, bf16[192,768]{1,0:T(8,128)(2,1)}) async-done(((bf16[48,2304]{1,0:T(8,128)(2,1)}, bf16[48,768]{1,0:T(8,128)(2,1)}, bf16[48,3072]{1,0:T(8,128)(2,1)}, bf16[192,768]{1,0:T(8,128)(2,1)}), (bf16[48,2304]{1,0:T(8,128)(2,1)}, bf16[48,768]{1,0:T(8,128)(2,1)}, ...) | async-done | bytes 884752 | tf_op jit(solution)/shard_map/psum | solution.py:271
  (229 shorter events, 57.1 us)
Async XLA Ops:
  7.2 70.6 %all-gather.7.cloned.1.call-start = ((), (), s32[]{:S(2)}) async-start(), calls=%async_computation.6 | async-start | bytes 3760128 | tf_op jit(solution)/shard_map/all_gather | solution.py:162
  7.9 183.2 %all-gather.9.cloned.1.call-start = ((), (), s32[]{:S(2)}) async-start(), calls=%async_computation.7 | async-start | bytes 1253376 | tf_op jit(solution)/shard_map/all_gather | solution.py:163
  8.7 187.8 %all-gather.11.cloned.1.call-start = ((), (), s32[]{:S(2)}) async-start(), calls=%async_computation.8 | async-start | bytes 5013504 | tf_op jit(solution)/shard_map/all_gather | solution.py:164
  9.4 200.7 %all-gather.13.cloned.1.call-start = ((), (), s32[]{:S(2)}) async-start(), calls=%async_computation.9 | async-start | bytes 5013504 | tf_op jit(solution)/shard_map/all_gather | solution.py:165
  10.0 606.2 %reduce-scatter.13.cloned.1.call-start = ((), (), s32[]{:S(2)}) async-start(), calls=%async_computation.11 | async-start | bytes 1253376 | tf_op jit(solution)/shard_map/reduce_scatter | solution.py:254
  55.0 46.0 %copy-start.18 = (f32[1024,64]{0,1:T(8,128)}, f32[1024,64]{0,1:T(8,128)S(1)}, u32[]{:S(2)}) copy-start(f32[1024,64]{0,1:T(8,128)S(1)} %get-tuple-element.546) | copy-start | bytes 786436
  55.0 2.6 copy-start.14
  56.9 20.9 %copy-start.2 = (bf16[1024,768]{0,1:T(8,128)(2,1)}, bf16[1024,768]{0,1:T(8,128)(2,1)S(1)}, u32[]{:S(2)}) copy-start(bf16[1024,768]{0,1:T(8,128)(2,1)S(1)} %copy.80) | copy-start | bytes 4718596
  56.9 2.4 copy-start.50
  57.2 20.7 %copy-start.32 = (f32[1024]{0:T(1024)}, f32[1024]{0:T(1024)S(1)}, u32[]{:S(2)}) copy-start(f32[1024]{0:T(1024)S(1)} %broadcast_multiply_fusion.7) | copy-start | bytes 12292
  57.6 20.2 %copy-start.36 = (f32[1024]{0:T(1024)}, f32[1024]{0:T(1024)S(1)}, u32[]{:S(2)}) copy-start(f32[1024]{0:T(1024)S(1)} %add_rsqrt_fusion.1) | copy-start | bytes 12292
  77.8 6.3 copy-start.34
  77.8 6.3 copy-start.47
  91.2 9.5 %copy-start.5 = (f32[1024,768]{0,1:T(8,128)}, f32[1024,768]{0,1:T(8,128)S(1)}, u32[]{:S(2)}) copy-start(f32[1024,768]{0,1:T(8,128)S(1)} %copy.85) | copy-start | bytes 9437188
  100.7 1.9 copy-start.6
  100.7 1.9 copy-start.20
  102.6 4.3 copy-start.24
  185.2 1.1 copy-start.25
  186.4 4.7 copy-start.3
  194.4 1.7 copy-start.8
  194.4 2.1 copy-start.40
  194.4 2.1 copy-start.45
  194.5 43.9 %copy-start.38 = (f32[1024]{0:T(1024)}, f32[1024]{0:T(1024)S(1)}, u32[]{:S(2)}) copy-start(f32[1024]{0:T(1024)S(1)} %broadcast_multiply_fusion.6) | copy-start | bytes 12292
  196.5 41.9 %copy-start.42 = (f32[1024]{0:T(1024)}, f32[1024]{0:T(1024)S(1)}, u32[]{:S(2)}) copy-start(f32[1024]{0:T(1024)S(1)} %add_rsqrt_fusion) | copy-start | bytes 12292
  196.5 13.6 %copy-start.16 = (bf16[1024,768]{0,1:T(8,128)(2,1)S(1)}, bf16[1024,768]{0,1:T(8,128)(2,1)}, u32[]{:S(2)}) copy-start(bf16[1024,768]{0,1:T(8,128)(2,1)} %copy.90) | copy-start | bytes 4718596
  210.1 12.8 %copy-start.52 = (bf16[768,3072]{1,0:T(8,128)(2,1)S(1)}, bf16[768,3072]{1,0:T(8,128)(2,1)}, u32[]{:S(2)}) copy-start(bf16[768,3072]{1,0:T(8,128)(2,1)} %all-gather.11.cloned.1.call-done) | copy-start | bytes 14155780
  222.9 7.3 copy-start.55
  233.8 4.6 copy-start.9
  233.8 4.7 copy-start.10
  251.0 1.7 copy-start.22
  252.7 4.0 copy-start.54
  256.6 359.5 %reduce-scatter.11.cloned.1.call-start = ((), (), s32[]{:S(2)}) async-start(), calls=%async_computation.10 | async-start | bytes 3760128 | tf_op jit(solution)/shard_map/reduce_scatter | solution.py:251
  266.6 11.6 %copy-start.13 = (bf16[1024,12,64]{0,2,1:T(8,128)(2,1)S(1)}, bf16[1024,12,64]{0,2,1:T(8,128)(2,1)}, u32[]{:S(2)}) copy-start(bf16[1024,12,64]{0,2,1:T(8,128)(2,1)} %get-tuple-element.783) | copy-start | bytes 4718596 | tf_op jit(solution)/shard_map/while/body/eval_jaxpr/while
  340.8 9.0 copy-start.1
  385.1 11.5 %copy-start.13 = (bf16[1024,12,64]{0,2,1:T(8,128)(2,1)S(1)}, bf16[1024,12,64]{0,2,1:T(8,128)(2,1)}, u32[]{:S(2)}) copy-start(bf16[1024,12,64]{0,2,1:T(8,128)(2,1)} %get-tuple-element.783) | copy-start | bytes 4718596 | tf_op jit(solution)/shard_map/while/body/eval_jaxpr/while
  459.8 9.9 %copy-start.1 = (f32[1,512,12,64]{1,3,2,0:T(8,128)S(1)}, f32[1,512,12,64]{1,3,2,0:T(8,128)}, u32[]{:S(2)}) copy-start(f32[1,512,12,64]{1,3,2,0:T(8,128)} %multiply_bitcast_fusion.3) | copy-start | bytes 4718596 | tf_op jit(solution)/shard_map/while/body/eval_jaxpr/while
  500.2 3.5 copy-start.7
  507.4 1.9 copy-start.11
  507.4 1.9 copy-start.21
  509.8 1.9 copy-start
  514.0 1.3 copy-start.28
  514.4 2.1 copy-start.4
  514.4 2.4 copy-start.26
  514.4 2.4 copy-start.33
  514.4 2.4 copy-start.35
  514.4 2.4 copy-start.37
  514.4 2.4 copy-start.48
  515.3 1.2 copy-start.30
  522.8 145.1 %reduce-scatter.15.cloned.1.call-start = ((), (), s32[]{:S(2)}) async-start(), calls=%async_computation.12 | async-start | bytes 5013504 | tf_op jit(solution)/shard_map/reduce_scatter | solution.py:257
  533.3 1.5 copy-start.17
  533.3 213.2 %reduce-scatter.17.cloned.1.call-start = ((), (), s32[]{:S(2)}) async-start(), calls=%async_computation.13 | async-start | bytes 5013504 | tf_op jit(solution)/shard_map/reduce_scatter | solution.py:260
  545.7 3.2 copy-start.15
  545.7 257.4 %reduce-scatter.21.cloned.1.call-start = ((), (), s32[]{:S(2)}) async-start(), calls=%async_computation.15 | async-start | bytes 208896
  549.2 5.3 copy-start.12
  549.2 5.3 copy-start.51
  554.5 6.9 copy-start.49
  554.5 6.9 copy-start.44
  554.5 6.9 copy-start.27
  554.5 6.9 copy-start.29
  554.5 6.9 copy-start.31
  554.5 6.9 copy-start.53
  571.4 43.2 %copy-start.23 = (bf16[1024,768]{0,1:T(8,128)(2,1)S(1)}, bf16[1024,768]{0,1:T(8,128)(2,1)}, u32[]{:S(2)}) copy-start(bf16[1024,768]{0,1:T(8,128)(2,1)} %get-tuple-element.534) | copy-start | bytes 4718596
  574.5 284.9 %reduce-scatter.19.cloned.1.call-start = ((), (), s32[]{:S(2)}) async-start(), calls=%async_computation.14 | async-start | bytes 208896
  576.2 321.4 %all-reduce.4.cloned.1.call-start = ((), (), s32[]{:S(2)}) async-start(), calls=%async_computation.16 | async-start | bytes 1769472 | tf_op jit(solution)/shard_map/psum | solution.py:271
  (5 other events, 3.7 us)
Sparse Core Ops, SparseCore 0:
  10.3 49.9 all-gather.6
  62.5 36.9 all-gather.8
  101.7 51.9 all-gather.10
  155.9 51.6 all-gather.12
  256.8 56.7 reduce-scatter.12
  522.9 66.7 reduce-scatter.10
  593.5 74.3 reduce-scatter.14
  671.8 74.6 reduce-scatter.16
  750.6 52.4 reduce-scatter.20
  807.0 52.3 reduce-scatter.18
  861.9 35.5 all-reduce.3
where the time goes:
time: 926 us; the launch traced here: 911 us
  matrix products  279 us (30%)
  waiting for transfers between devices  267 us (29%)
  local copies, waits for them, and re-layouts  133 us (14%)
  other arithmetic  125 us (13%)
  blocking collectives  84.4 us (9%)
  between operations  15.7 us (2%)
    unnamed x13, waiting for transfers between devices  106 us
    reduce_scatter x1, waiting for transfers between devices, local(): lax.psum_scatter(local_grads[3].astype(jnp.bfloat16), 'shard', scatter_di...  78.5 us
    dynamic_update_slice x4, local copies, waits for them, and re-layouts, attend_backward(): lax.scan(one_block, (zero_rows, zero_rows), jnp.arange(block_count, dtype...  60.6 us
    reduce_scatter x1, waiting for transfers between devices, local(): lax.psum_scatter(local_grads[2].astype(jnp.bfloat16), 'shard', scatter_di...  51.8 us
    dot_general x4, matrix products, block_scores(): jnp.einsum('qhd,khd->hqk', query_block, key_rows, preferred_element_type=...  47.1 us
    convert_element_type x2, other arithmetic, one_block(): grad_scores = (attn_probs * (grad_probs - delta_sum)).astype(jnp.bfloat16)  42.5 us
    psum x1, blocking collectives, local(): grad_mix = lax.psum(partial_mix, ('rep', 'shard'))  38.4 us
    dot_general x2, matrix products, one_block(): jnp.einsum('qhd,khd->hqk', grad_block, value_rows, preferred_element_type...  36.3 us
  transfers between devices with their start and end apart: 11, of which 5 were waited for; matrix products, arithmetic and copies ran while one was open for 52% of the time, Pallas kernels for 0%

commit v1 on v0

--- a/solution.py
+++ b/solution.py
@@ -268,7 +268,7 @@
         ).astype(jnp.float32),
     )
     owned = (
-        lax.psum(owned[0].astype(jnp.bfloat16), "rep").astype(jnp.float32),
+        jnp.sum(lax.all_gather(owned[0].astype(jnp.bfloat16), "rep"), axis=0).astype(jnp.float32),
         lax.psum(owned[1].astype(jnp.bfloat16), "rep").astype(jnp.float32),
         lax.psum(owned[2].astype(jnp.bfloat16), "rep").astype(jnp.float32),
         lax.psum(owned[3].astype(jnp.bfloat16), "rep").astype(jnp.float32),

time: 926 us -> 795 us (0.86)
  waiting for transfers between devices: 267 us -> 128 us
    reduce_scatter x1, waiting for transfers between devices: 78.5 us -> 0.02 us  [local(): lax.psum_scatter(local_grads[3].astype(jnp.bfloat16), 'shard', scatter_di...]
    unnamed x13, waiting for transfers between devices: 106 us -> 37.9 us
    reduce_scatter x1, waiting for transfers between devices: 0.01 us -> 64.1 us  [local(): lax.psum_scatter(local_grads[0].astype(jnp.bfloat16), 'shard', scatter_di...]
    reduce_scatter x1, waiting for transfers between devices: 51.8 us -> 0.01 us  [local(): lax.psum_scatter(local_grads[2].astype(jnp.bfloat16), 'shard', scatter_di...]
    unnamed x118 -> x98, local copies, waits for them, and re-layouts: 27.2 us -> 26.6 us
  transfers between devices with their start and end apart: 11 -> 11, of which waited for: 5 -> 3; matrix products, arithmetic and copies ran while one was open for 52% -> 61% of each run, Pallas kernels for 0% -> 0%
where the time goes in v1:
time: 795 us; the launch traced here: 781 us
  matrix products  281 us (35%)
  local copies, waits for them, and re-layouts  132 us (17%)
  waiting for transfers between devices  128 us (16%)
  other arithmetic  124 us (16%)
  blocking collectives  91.6 us (12%)
  between operations  15.3 us (2%)
    reduce_scatter x1, waiting for transfers between devices, local(): lax.psum_scatter(local_grads[0].astype(jnp.bfloat16), 'shard', scatter_di...  64.1 us
    dynamic_update_slice x4, local copies, waits for them, and re-layouts, attend_backward(): lax.scan(one_block, (zero_rows, zero_rows), jnp.arange(block_count, dtype...  60.9 us
    dot_general x4, matrix products, block_scores(): jnp.einsum('qhd,khd->hqk', query_block, key_rows, preferred_element_type=...  46.9 us
    convert_element_type x2, other arithmetic, one_block(): grad_scores = (attn_probs * (grad_probs - delta_sum)).astype(jnp.bfloat16)  44.5 us
    psum x1, blocking collectives, local(): grad_mix = lax.psum(partial_mix, ('rep', 'shard'))  38.7 us
    unnamed x13, waiting for transfers between devices  37.9 us
    dot_general x2, matrix products, one_block(): jnp.einsum('qhd,khd->hqk', grad_block, value_rows, preferred_element_type...  37 us
    dot_general x2, matrix products, one_block(): jnp.einsum('hqk,qhd->khd', attn_probs.astype(jnp.bfloat16), grad_block, p...  28.3 us
  transfers between devices with their start and end apart: 11, of which 3 were waited for; matrix products, arithmetic and copies ran while one was open for 61% of the time, Pallas kernels for 0%

profile of v1, /device:TPU:0, one launch (start us, length us, event | category | flops | bytes accessed | tf_op | source)
XLA Modules:
  0.0 780.6 jit_solution(17351879389953660098)
XLA Ops:
  11.9 23.4 %all-gather.1 = bf16[16,48,2]{1,2,0:T(2,128)(2,1)S(1)} all-gather(bf16[1,48,2]{1,2,0:T(2,128)(2,1)} %bitcast.172), channel_id=1, replica_groups=mesh['rep'=2,'shard'=16] {'shard'}, dimensions={0}, use_global_device_ids=true | all-gather | bytes 3264 | tf_op jit(solution)/shard_map/all_gather | solution.py:166
  35.5 17.7 %all-gather.2 = bf16[16,48,2]{1,2,0:T(2,128)(2,1)S(1)} all-gather(bf16[1,48,2]{1,2,0:T(2,128)(2,1)} %bitcast.173), channel_id=1, replica_groups=mesh['rep'=2,'shard'=16] {'shard'}, dimensions={0}, use_global_device_ids=true | all-gather | bytes 3264 | tf_op jit(solution)/shard_map/all_gather | solution.py:167
  55.0 1.8 copy.80
  59.3 9.4 %fusion.43 = f32[1,1024,768]{2,0,1:T(1,128)} fusion(bf16[4,1024,768]{2,1,0:T(8,128)(2,1)} %param.16, f32[5]{0:T(128)S(1)} %copy-done.40), kind=kOutput, calls=%fused_computation.65 | convolution fusion | flops 6291456 | bytes 9437204 | tf_op jit(solution)/shard_map/k,ktd->td/dot_general | solution.py:198
  68.7 8.5 %copy.101 = f32[1,1024,768]{1,2,0:T(8,128)} copy(f32[1,1024,768]{2,0,1:T(1,128)} %fusion.43) | data formatting | bytes 6291456 | tf_op jit(solution)/shard_map/k,ktd->td/dot_general | solution.py:198
  77.8 6.3 fusion.79
  85.4 3.1 fusion.82
  88.5 2.6 copy.85
  91.1 3.7 copy.87
  94.8 3.5 copy.83
  98.3 2.3 fusion.69
  102.5 4.3 fusion.62
  106.8 77.9 %while.52 = (s32[]{:T(128)}, bf16[2,512,12,64]{1,3,2,0:T(8,128)(2,1)S(1)}, f32[2,12,512]{2,1,0:T(8,128)S(1)}, s32[2]{0:T(128)S(1)}, s32[]{:T(128)}, /*index=5*/s...) while((s32[]{:T(128)}, ...), condition=%wide.region_5.6_spmd.clone.clone, body=%wide.region_2.5_spmd.clone.clone.sunk | while | flops 1681784320 | bytes 82558176 | solution.py:92
  109.9 12.0 %fusion.130 = (f32[12,512]{1,0:T(8,128)S(1)}, f32[12,512,1024]{2,1,0:T(8,128)}) fusion(pred[512,1024]{1,0:T(8,128)(4,1)S(1)} %fusion.129, bf16[1024,12,64]{0,2,1:T(8,128)(2,1)S(1)} %get-tuple-element.732, bf16[1024,12,64]{0,2,1:T(8,128)(2,1)} %get-tuple-element.731, s32[]{:T(128)S(6)} %select_n.68), kind=kOutput, calls=%fused_computation.5.clone.1 | convolution fusion | flops 824174592 | bytes 28073988 | tf_op jit(solution)/shard_map/while/body/eval_jaxpr/while/body/eval_jaxpr/qhd,khd->hqk/dot_general | solution.py:67
  121.9 12.1 %exponential_reduce_fusion.2 = f32[12,512]{1,0:T(8,128)S(1)} fusion(f32[12,512,1024]{2,1,0:T(8,128)} %get-tuple-element.681, f32[12,512]{1,0:T(8,128)S(1)} %get-tuple-element.682, pred[512,1024]{1,0:T(8,128)(4,1)S(1)} %fusion.129), kind=kLoop, calls=%fused_computation.3.clone.1 | loop fusion | flops 25159680 | bytes 25739264 | tf_op jit(solution)/shard_map/while/body/eval_jaxpr/while/body/eval_jaxpr/reduce_sum | solution.py:85
  134.0 11.8 %fusion.131 = bf16[2,512,12,64]{1,3,2,0:T(8,128)(2,1)S(1)} fusion(bf16[2,512,12,64]{1,3,2,0:T(8,128)(2,1)S(1)} %get-tuple-element.713, s32[]{:T(128)S(6)} %copy.143, bf16[1024,12,64]{0,2,1:T(8,128)(2,1)} %get-tuple-element.733, f32[12,512,1024]{2,1,0:T(8,128)} %get-tuple-element.681, f32[12,512]{1,0:T(8,128)S(1)} %get-tuple-element.683, ...), kind=kOutput, calls=%fused_computation.12.clone.1 | convolution fusion | flops 830865408 | bytes 28082180 | tf_op jit(solution)/shard_map/while/body/eval_jaxpr/while/body/eval_jaxpr/hqk,khd->qhd/dot_general | solution.py:87
  148.9 11.9 %fusion.130 = (f32[12,512]{1,0:T(8,128)S(1)}, f32[12,512,1024]{2,1,0:T(8,128)}) fusion(pred[512,1024]{1,0:T(8,128)(4,1)S(1)} %fusion.129, bf16[1024,12,64]{0,2,1:T(8,128)(2,1)S(1)} %get-tuple-element.732, bf16[1024,12,64]{0,2,1:T(8,128)(2,1)} %get-tuple-element.731, s32[]{:T(128)S(6)} %select_n.68), kind=kOutput, calls=%fused_computation.5.clone.1 | convolution fusion | flops 824174592 | bytes 28073988 | tf_op jit(solution)/shard_map/while/body/eval_jaxpr/while/body/eval_jaxpr/qhd,khd->hqk/dot_general | solution.py:67
  160.8 12.0 %exponential_reduce_fusion.2 = f32[12,512]{1,0:T(8,128)S(1)} fusion(f32[12,512,1024]{2,1,0:T(8,128)} %get-tuple-element.681, f32[12,512]{1,0:T(8,128)S(1)} %get-tuple-element.682, pred[512,1024]{1,0:T(8,128)(4,1)S(1)} %fusion.129), kind=kLoop, calls=%fused_computation.3.clone.1 | loop fusion | flops 25159680 | bytes 25739264 | tf_op jit(solution)/shard_map/while/body/eval_jaxpr/while/body/eval_jaxpr/reduce_sum | solution.py:85
  172.8 11.6 %fusion.131 = bf16[2,512,12,64]{1,3,2,0:T(8,128)(2,1)S(1)} fusion(bf16[2,512,12,64]{1,3,2,0:T(8,128)(2,1)S(1)} %get-tuple-element.713, s32[]{:T(128)S(6)} %copy.143, bf16[1024,12,64]{0,2,1:T(8,128)(2,1)} %get-tuple-element.733, f32[12,512,1024]{2,1,0:T(8,128)} %get-tuple-element.681, f32[12,512]{1,0:T(8,128)S(1)} %get-tuple-element.683, ...), kind=kOutput, calls=%fused_computation.12.clone.1 | convolution fusion | flops 830865408 | bytes 28082180 | tf_op jit(solution)/shard_map/while/body/eval_jaxpr/while/body/eval_jaxpr/hqk,khd->qhd/dot_general | solution.py:87
  185.9 3.1 copy.88
  190.6 3.3 fusion.84
  196.0 13.5 %multiply_convert_fusion.1 = (bf16[1024,3072]{1,0:T(8,128)(2,1)}, f32[1024,3072]{1,0:T(8,128)}) fusion(bf16[768,3072]{1,0:T(8,128)(2,1)} %all-gather.12.cloned.1.call-done, f32[1024,768]{0,1:T(8,128)} %copy-done.7, f32[768]{0:T(1024)S(1)} %copy-done.38, f32[768]{0:T(1024)S(1)} %copy-done.34, f32[1024]{0:T(1024)S(1)} %add_rsqrt_fusion, ...), kind=kOutput, calls=%fused_computation.62 | convolution fusion | flops 4851499008 | bytes 26753024 | tf_op jit(solution)/shard_map/dot_general | solution.py:194
  209.5 13.1 %fusion.42 = bf16[1024,3072]{1,0:T(8,128)(2,1)S(1)} fusion(f32[1024,3072]{1,0:T(8,128)} %get-tuple-element.552, bf16[3072,768]{1,0:T(8,128)(2,1)} %all-gather.14.cloned.1.call-done, bf16[1024,768]{0,1:T(8,128)(2,1)S(1)} %copy-done.16, f32[]{:T(128)} %bitcast.4), kind=kOutput, calls=%fused_computation.60 | convolution fusion | flops 4865654784 | bytes 25165828 | tf_op jit(solution)/shard_map/td,fd->tf/dot_general | solution.py:214
  222.6 7.3 fusion.85
  229.9 3.6 copy.91
  233.5 4.6 multiply_reduce_fusion.2
  238.2 12.5 %multiply_reduce_fusion.3 = (f32[]{:T(128)}, bf16[1024,768]{0,1:T(8,128)(2,1)}, f32[1024,768]{0,1:T(8,128)S(1)}) fusion(bf16[1024,768]{0,1:T(8,128)(2,1)S(1)} %copy-done.16, f32[]{:T(128)} %bitcast.4, f32[1,1024,768]{1,2,0:T(8,128)} %copy.101, f32[1024]{0:T(1024)S(1)} %broadcast_multiply_fusion.4, f32[1024,768]{0,1:T(8,128)S(1)} %copy-done.8, ...), kind=kOutput, calls=%fused_computation.104 | convolution fusion | flops 4844421120 | bytes 26758152 | tf_op jit(solution)/shard_map/dot_general | solution.py:197
  252.4 3.8 convolution_convert_fusion.4
  256.3 9.9 %convolution_convert_fusion.1 = bf16[768,3072]{1,0:T(8,128)(2,1)} fusion(bf16[1024,3072]{1,0:T(8,128)(2,1)} %copy-done.45, f32[1024,768]{0,1:T(8,128)} %copy-done.7, f32[768]{0:T(1024)S(1)} %copy-done.38, f32[768]{0:T(1024)S(1)} %copy-done.34, f32[1024]{0:T(1024)S(1)} %add_rsqrt_fusion, f32[1024]{0:T(1024)S(1)} %broadcast_multiply_fusion.6), kind=kOutput, calls=%fused_computation.68 | convolution fusion | flops 4838129664 | bytes 14170112 | tf_op jit(solution)/shard_map/td,tf->df/dot_general | solution.py:218
  266.3 10.6 %convolution_convert_fusion = bf16[3072,768]{1,0:T(8,128)(2,1)} fusion(bf16[1024,3072]{1,0:T(8,128)(2,1)} %get-tuple-element.551, bf16[1024,768]{0,1:T(8,128)(2,1)S(1)} %copy-done.16, f32[]{:T(128)} %bitcast.4), kind=kOutput, calls=%fused_computation.67 | convolution fusion | flops 4836556800 | bytes 12582916 | tf_op jit(solution)/shard_map/tf,td->fd/dot_general | solution.py:213
  278.1 4.6 convolution_convert_fusion.3
  282.7 242.5 %while.53 = (s32[]{:T(128)}, f32[1024,12,64]{0,2,1:T(8,128)}, f32[1024,12,64]{0,2,1:T(8,128)}, f32[2,512,12,64]{1,0,3,2:T(2,128)}, s32[2]{0:T(128)S(1)}, /*index...) while((s32[]{:T(128)}, f32[1024,12,64]{0,2,1:T(8,128)}, ...), condition=%wide.region_12.13_spmd.clone.clone, body=%wide.region_10.12_spmd.clone.clone.sunk | while | flops 4126801408 | bytes 231923056 | solution.py:136
  287.9 11.4 %fusion.141 = f32[12,512,1024]{2,1,0:T(8,128)} fusion(bf16[1024,12,64]{0,2,1:T(8,128)(2,1)S(1)} %get-tuple-element.780, bf16[1024,12,64]{0,2,1:T(8,128)(2,1)} %get-tuple-element.777, s32[]{:T(128)S(6)} %select_n.72), kind=kOutput, calls=%fused_computation.40.clone.1 | convolution fusion | flops 805306368 | bytes 27525124 | tf_op jit(solution)/shard_map/while/body/eval_jaxpr/while/body/eval_jaxpr/qhd,khd->hqk/dot_general | solution.py:67
  299.3 13.5 %bitcast_add_fusion.7 = f32[1024,12,64]{0,2,1:T(8,128)} fusion(f32[1024,12,64]{0,2,1:T(8,128)} %get-tuple-element.757, f32[12,512,1024]{2,1,0:T(8,128)} %fusion.141, f32[12,512]{1,0:T(8,128)S(1)} %dynamic-slice_bitcast_fusion.2, pred[512,1024]{1,0:T(8,128)(4,1)S(1)} %fusion.143, pred[]{:T(512)S(6)} %compare.3, ...), kind=kOutput, calls=%fused_computation.31.clone.1 | convolution fusion | flops 832045056 | bytes 32800772 | tf_op jit(solution)/shard_map/while/body/eval_jaxpr/while/body/eval_jaxpr/hqk,qhd->khd/dot_general | solution.py:127
  312.7 18.9 %multiply_reduce_fusion.9 = (f32[12,512]{1,0:T(8,128)S(1)}, f32[12,512,1024]{2,1,0:T(8,128)}) fusion(f32[12,512,1024]{2,1,0:T(8,128)} %fusion.141, f32[12,512]{1,0:T(8,128)S(1)} %dynamic-slice_bitcast_fusion.2, pred[512,1024]{1,0:T(8,128)(4,1)S(1)} %fusion.143, bf16[1024,12,64]{0,2,1:T(8,128)(2,1)} %get-tuple-element.783, ...), kind=kOutput, calls=%fused_computation.26.clone.1 | convolution fusion | flops 836757504 | bytes 53264388 | tf_op jit(solution)/shard_map/while/body/eval_jaxpr/while/body/eval_jaxpr/qhd,khd->hqk/dot_general | solution.py:111
  331.6 22.8 %multiply_convert_fusion.6 = bf16[12,512,1024]{2,1,0:T(8,128)(2,1)} fusion(f32[12,512,1024]{2,1,0:T(8,128)} %get-tuple-element.697, f32[12,512,1024]{2,1,0:T(8,128)} %fusion.141, f32[12,512]{1,0:T(8,128)S(1)} %get-tuple-element.698, f32[12,512]{1,0:T(8,128)S(1)} %dynamic-slice_bitcast_fusion.2, pred[512,1024]{1,0:T(8,128)(4,1)S(1)} %fusion.143), kind=kLoop, calls=%fused_computation.25.clone.1 | loop fusion | flops 37748736 | bytes 63488000 | tf_op jit(solution)/shard_map/while/body/eval_jaxpr/while/body/eval_jaxpr/convert_element_type | solution.py:115
  354.4 9.7 %multiply_bitcast_fusion.3 = f32[1,512,12,64]{1,3,2,0:T(8,128)} fusion(bf16[12,512,1024]{2,1,0:T(8,128)(2,1)} %multiply_convert_fusion.6, bf16[1024,12,64]{0,2,1:T(8,128)(2,1)S(1)} %get-tuple-element.780), kind=kOutput, calls=%fused_computation.35.clone.1 | convolution fusion | flops 805699584 | bytes 15728640 | tf_op jit(solution)/shard_map/while/body/eval_jaxpr/while/body/eval_jaxpr/hqk,khd->qhd/dot_general | solution.py:117
  364.1 9.0 %bitcast_add_fusion.6 = f32[1024,12,64]{0,2,1:T(8,128)} fusion(f32[1024,12,64]{0,2,1:T(8,128)} %get-tuple-element.756, bf16[12,512,1024]{2,1,0:T(8,128)(2,1)} %multiply_convert_fusion.6, pred[]{:T(512)S(6)} %compare.3, bf16[1024,12,64]{0,2,1:T(8,128)(2,1)} %get-tuple-element.777, s32[]{:T(128)S(6)} %select_n.72), kind=kOutput, calls=%fused_computation.32.clone.1 | convolution fusion | flops 807665664 | bytes 19660804 | tf_op jit(solution)/shard_map/while/body/eval_jaxpr/while/body/eval_jaxpr/hqk,qhd->khd/dot_general | solution.py:122
  374.7 28.8 %dynamic_update_slice.41 = f32[2,512,12,64]{1,0,3,2:T(2,128)} dynamic-update-slice(f32[2,512,12,64]{1,0,3,2:T(2,128)} %get-tuple-element.758, f32[1,512,12,64]{1,0,3,2:T(1,128)S(1)} %copy.136, s32[]{:T(128)S(6)} %copy.153, s32[]{:T(128)} %constant.130.clone.1..sunk.1, s32[]{:T(128)} %constant.130.clone.1..sunk.1, s32[]{:T(128)} %constant.130.clone.1..sunk.1) | dynamic-update-slice | bytes 3145732 | tf_op jit(solution)/shard_map/while/body/eval_jaxpr/while/body/jit(dynamic_update_index_in_dim)/dynamic_update_slice | solution.py:136
  408.5 11.6 %fusion.141 = f32[12,512,1024]{2,1,0:T(8,128)} fusion(bf16[1024,12,64]{0,2,1:T(8,128)(2,1)S(1)} %get-tuple-element.780, bf16[1024,12,64]{0,2,1:T(8,128)(2,1)} %get-tuple-element.777, s32[]{:T(128)S(6)} %select_n.72), kind=kOutput, calls=%fused_computation.40.clone.1 | convolution fusion | flops 805306368 | bytes 27525124 | tf_op jit(solution)/shard_map/while/body/eval_jaxpr/while/body/eval_jaxpr/qhd,khd->hqk/dot_general | solution.py:67
  420.1 14.9 %bitcast_add_fusion.7 = f32[1024,12,64]{0,2,1:T(8,128)} fusion(f32[1024,12,64]{0,2,1:T(8,128)} %get-tuple-element.757, f32[12,512,1024]{2,1,0:T(8,128)} %fusion.141, f32[12,512]{1,0:T(8,128)S(1)} %dynamic-slice_bitcast_fusion.2, pred[512,1024]{1,0:T(8,128)(4,1)S(1)} %fusion.143, pred[]{:T(512)S(6)} %compare.3, ...), kind=kOutput, calls=%fused_computation.31.clone.1 | convolution fusion | flops 832045056 | bytes 32800772 | tf_op jit(solution)/shard_map/while/body/eval_jaxpr/while/body/eval_jaxpr/hqk,qhd->khd/dot_general | solution.py:127
  435.0 18.1 %multiply_reduce_fusion.9 = (f32[12,512]{1,0:T(8,128)S(1)}, f32[12,512,1024]{2,1,0:T(8,128)}) fusion(f32[12,512,1024]{2,1,0:T(8,128)} %fusion.141, f32[12,512]{1,0:T(8,128)S(1)} %dynamic-slice_bitcast_fusion.2, pred[512,1024]{1,0:T(8,128)(4,1)S(1)} %fusion.143, bf16[1024,12,64]{0,2,1:T(8,128)(2,1)} %get-tuple-element.783, ...), kind=kOutput, calls=%fused_computation.26.clone.1 | convolution fusion | flops 836757504 | bytes 53264388 | tf_op jit(solution)/shard_map/while/body/eval_jaxpr/while/body/eval_jaxpr/qhd,khd->hqk/dot_general | solution.py:111
  453.1 21.8 %multiply_convert_fusion.6 = bf16[12,512,1024]{2,1,0:T(8,128)(2,1)} fusion(f32[12,512,1024]{2,1,0:T(8,128)} %get-tuple-element.697, f32[12,512,1024]{2,1,0:T(8,128)} %fusion.141, f32[12,512]{1,0:T(8,128)S(1)} %get-tuple-element.698, f32[12,512]{1,0:T(8,128)S(1)} %dynamic-slice_bitcast_fusion.2, pred[512,1024]{1,0:T(8,128)(4,1)S(1)} %fusion.143), kind=kLoop, calls=%fused_computation.25.clone.1 | loop fusion | flops 37748736 | bytes 63488000 | tf_op jit(solution)/shard_map/while/body/eval_jaxpr/while/body/eval_jaxpr/convert_element_type | solution.py:115
  474.9 9.7 %multiply_bitcast_fusion.3 = f32[1,512,12,64]{1,3,2,0:T(8,128)} fusion(bf16[12,512,1024]{2,1,0:T(8,128)(2,1)} %multiply_convert_fusion.6, bf16[1024,12,64]{0,2,1:T(8,128)(2,1)S(1)} %get-tuple-element.780), kind=kOutput, calls=%fused_computation.35.clone.1 | convolution fusion | flops 805699584 | bytes 15728640 | tf_op jit(solution)/shard_map/while/body/eval_jaxpr/while/body/eval_jaxpr/hqk,khd->qhd/dot_general | solution.py:117
  484.6 9.8 %bitcast_add_fusion.6 = f32[1024,12,64]{0,2,1:T(8,128)} fusion(f32[1024,12,64]{0,2,1:T(8,128)} %get-tuple-element.756, bf16[12,512,1024]{2,1,0:T(8,128)(2,1)} %multiply_convert_fusion.6, pred[]{:T(512)S(6)} %compare.3, bf16[1024,12,64]{0,2,1:T(8,128)(2,1)} %get-tuple-element.777, s32[]{:T(128)S(6)} %select_n.72), kind=kOutput, calls=%fused_computation.32.clone.1 | convolution fusion | flops 807665664 | bytes 19660804 | tf_op jit(solution)/shard_map/while/body/eval_jaxpr/while/body/eval_jaxpr/hqk,qhd->khd/dot_general | solution.py:122
  496.0 28.8 %dynamic_update_slice.41 = f32[2,512,12,64]{1,0,3,2:T(2,128)} dynamic-update-slice(f32[2,512,12,64]{1,0,3,2:T(2,128)} %get-tuple-element.758, f32[1,512,12,64]{1,0,3,2:T(1,128)S(1)} %copy.136, s32[]{:T(128)S(6)} %copy.153, s32[]{:T(128)} %constant.130.clone.1..sunk.1, s32[]{:T(128)} %constant.130.clone.1..sunk.1, s32[]{:T(128)} %constant.130.clone.1..sunk.1) | dynamic-update-slice | bytes 3145732 | tf_op jit(solution)/shard_map/while/body/eval_jaxpr/while/body/jit(dynamic_update_index_in_dim)/dynamic_update_slice | solution.py:136
  525.2 3.4 convert.34
  528.7 3.7 broadcast_in_dim.95
  541.8 5.8 fusion.86
  548.4 3.6 copy.94
  552.1 2.9 fusion.57
  556.3 7.7 convolution_convert_fusion.2
  564.1 3.2 copy.95
  567.5 5.1 multiply_reduce_fusion.1
  573.3 5.8 broadcast_multiply_fusion
  579.2 38.7 %psum.42 = f32[5]{0:T(128)} all-reduce(f32[5]{0:T(128)S(1)} %pad_maximum_fusion.7), channel_id=1, replica_groups=mesh['rep'=2,'shard'=16] {'rep','shard'}, use_global_device_ids=true, to_apply=%region_16.17 | all-reduce | flops 5 | bytes 40 | tf_op jit(solution)/shard_map/psum | solution.py:204
  619.5 5.5 fusion.56
  625.0 3.6 copy.99
  629.4 35.2 %reduce-scatter.19.cloned.1.call-done = bf16[48,2]{1,0:T(8,128)(2,1)} async-done(((bf16[768,2]{1,0:T(8,128)(2,1)}), bf16[48,2]{1,0:T(8,128)(2,1)}) %reduce-scatter.19.cloned.1.call-update) | async-done | bytes 208
  665.4 4.9 all-reduce
  671.4 64.1 %reduce-scatter.11.cloned.1.call-done = bf16[48,2304]{1,0:T(8,128)(2,1)} async-done(((bf16[768,2304]{1,0:T(8,128)(2,1)}), bf16[48,2304]{1,0:T(8,128)(2,1)}) %reduce-scatter.11.cloned.1.call-update) | async-done | bytes 221200 | tf_op jit(solution)/shard_map/reduce_scatter | solution.py:251
  735.5 6.8 all-gather
  743.2 25.5 %all-reduce.4.cloned.1.call-done = (bf16[48,768]{1,0:T(8,128)(2,1)}, bf16[48,3072]{1,0:T(8,128)(2,1)}, bf16[192,768]{1,0:T(8,128)(2,1)}) async-done(((bf16[48,768]{1,0:T(8,128)(2,1)}, bf16[48,3072]{1,0:T(8,128)(2,1)}, bf16[192,768]{1,0:T(8,128)(2,1)}), (bf16[48,768]{1,0:T(8,128)(2,1)}, bf16[48,3072]{1,0:T(8,128)(2,1)}, bf16[192,768]{1,0:T(8,128)(2,1)})) %all-reduce.4.cloned.1.call-update) | async-done | bytes 663568 | tf_op jit(solution)/shard_map/psum | solution.py:272
  770.2 1.8 convert_element_type.142
  (211 shorter events, 53.8 us)
Async XLA Ops:
  7.2 70.6 %all-gather.8.cloned.1.call-start = ((), (), s32[]{:S(2)}) async-start(), calls=%async_computation.6 | async-start | bytes 3760128 | tf_op jit(solution)/shard_map/all_gather | solution.py:162
  7.9 182.7 %all-gather.10.cloned.1.call-start = ((), (), s32[]{:S(2)}) async-start(), calls=%async_computation.7 | async-start | bytes 1253376 | tf_op jit(solution)/shard_map/all_gather | solution.py:163
  8.7 187.3 %all-gather.12.cloned.1.call-start = ((), (), s32[]{:S(2)}) async-start(), calls=%async_computation.8 | async-start | bytes 5013504 | tf_op jit(solution)/shard_map/all_gather | solution.py:164
  9.4 200.1 %all-gather.14.cloned.1.call-start = ((), (), s32[]{:S(2)}) async-start(), calls=%async_computation.9 | async-start | bytes 5013504 | tf_op jit(solution)/shard_map/all_gather | solution.py:165
  10.0 609.5 %reduce-scatter.13.cloned.1.call-start = ((), (), s32[]{:S(2)}) async-start(), calls=%async_computation.11 | async-start | bytes 1253376 | tf_op jit(solution)/shard_map/reduce_scatter | solution.py:254
  55.0 45.9 %copy-start.17 = (f32[1024,64]{0,1:T(8,128)}, f32[1024,64]{0,1:T(8,128)S(1)}, u32[]{:S(2)}) copy-start(f32[1024,64]{0,1:T(8,128)S(1)} %get-tuple-element.545) | copy-start | bytes 786436
  55.0 2.6 copy-start.14
  56.9 20.9 %copy-start.2 = (bf16[1024,768]{0,1:T(8,128)(2,1)}, bf16[1024,768]{0,1:T(8,128)(2,1)S(1)}, u32[]{:S(2)}) copy-start(bf16[1024,768]{0,1:T(8,128)(2,1)S(1)} %copy.80) | copy-start | bytes 4718596
  56.9 2.4 copy-start.40
  57.2 20.6 %copy-start.28 = (f32[1024]{0:T(1024)}, f32[1024]{0:T(1024)S(1)}, u32[]{:S(2)}) copy-start(f32[1024]{0:T(1024)S(1)} %broadcast_multiply_fusion.7) | copy-start | bytes 12292
  57.6 20.2 %copy-start.32 = (f32[1024]{0:T(1024)}, f32[1024]{0:T(1024)S(1)}, u32[]{:S(2)}) copy-start(f32[1024]{0:T(1024)S(1)} %add_rsqrt_fusion.1) | copy-start | bytes 12292
  77.8 6.3 copy-start.30
  77.8 6.3 copy-start.36
  91.1 9.5 %copy-start.5 = (f32[1024,768]{0,1:T(8,128)}, f32[1024,768]{0,1:T(8,128)S(1)}, u32[]{:S(2)}) copy-start(f32[1024,768]{0,1:T(8,128)S(1)} %copy.85) | copy-start | bytes 9437188
  100.6 1.9 copy-start.6
  100.6 1.9 copy-start.19
  102.5 4.3 copy-start.23
  184.7 1.1 copy-start.24
  185.9 4.7 copy-start.3
  193.9 1.7 copy-start.7
  193.9 2.1 copy-start.34
  193.9 2.1 copy-start.38
  196.0 13.5 %copy-start.16 = (bf16[1024,768]{0,1:T(8,128)(2,1)S(1)}, bf16[1024,768]{0,1:T(8,128)(2,1)}, u32[]{:S(2)}) copy-start(bf16[1024,768]{0,1:T(8,128)(2,1)} %copy.90) | copy-start | bytes 4718596
  209.5 13.1 %copy-start.42 = (bf16[768,3072]{1,0:T(8,128)(2,1)S(1)}, bf16[768,3072]{1,0:T(8,128)(2,1)}, u32[]{:S(2)}) copy-start(bf16[768,3072]{1,0:T(8,128)(2,1)} %all-gather.12.cloned.1.call-done) | copy-start | bytes 14155780
  222.6 7.3 copy-start.45
  233.5 4.6 copy-start.8
  233.5 4.7 copy-start.10
  250.8 1.6 copy-start.21
  256.3 363.2 %reduce-scatter.15.cloned.1.call-start = ((), (), s32[]{:S(2)}) async-start(), calls=%async_computation.12 | async-start | bytes 5013504 | tf_op jit(solution)/shard_map/reduce_scatter | solution.py:257
  266.2 353.3 %reduce-scatter.17.cloned.1.call-start = ((), (), s32[]{:S(2)}) async-start(), calls=%async_computation.13 | async-start | bytes 5013504 | tf_op jit(solution)/shard_map/reduce_scatter | solution.py:260
  276.8 1.3 copy-start.44
  276.8 351.7 %reduce-scatter.21.cloned.1.call-start = ((), (), s32[]{:S(2)}) async-start(), calls=%async_computation.15 | async-start | bytes 208896
  282.7 242.5 %copy-start.39 = (bf16[768]{0:T(1024)(128)(2,1)S(1)}, bf16[768]{0:T(1024)(128)(2,1)}, u32[]{:S(2)}) copy-start(bf16[768]{0:T(1024)(128)(2,1)} %get-tuple-element.553) | copy-start | bytes 4612
  282.7 242.6 %copy-start.35 = (bf16[768]{0:T(1024)(128)(2,1)S(1)}, bf16[768]{0:T(1024)(128)(2,1)}, u32[]{:S(2)}) copy-start(bf16[768]{0:T(1024)(128)(2,1)} %get-tuple-element.467) | copy-start | bytes 4612
  287.9 11.4 %copy-start.13 = (bf16[1024,12,64]{0,2,1:T(8,128)(2,1)S(1)}, bf16[1024,12,64]{0,2,1:T(8,128)(2,1)}, u32[]{:S(2)}) copy-start(bf16[1024,12,64]{0,2,1:T(8,128)(2,1)} %get-tuple-element.782) | copy-start | bytes 4718596 | tf_op jit(solution)/shard_map/while/body/eval_jaxpr/while
  364.1 9.0 %copy-start.1 = (f32[1,512,12,64]{1,3,2,0:T(8,128)S(1)}, f32[1,512,12,64]{1,3,2,0:T(8,128)}, u32[]{:S(2)}) copy-start(f32[1,512,12,64]{1,3,2,0:T(8,128)} %multiply_bitcast_fusion.3) | copy-start | bytes 4718596 | tf_op jit(solution)/shard_map/while/body/eval_jaxpr/while
  408.5 11.6 %copy-start.13 = (bf16[1024,12,64]{0,2,1:T(8,128)(2,1)S(1)}, bf16[1024,12,64]{0,2,1:T(8,128)(2,1)}, u32[]{:S(2)}) copy-start(bf16[1024,12,64]{0,2,1:T(8,128)(2,1)} %get-tuple-element.782) | copy-start | bytes 4718596 | tf_op jit(solution)/shard_map/while/body/eval_jaxpr/while
  484.6 9.8 %copy-start.1 = (f32[1,512,12,64]{1,3,2,0:T(8,128)S(1)}, f32[1,512,12,64]{1,3,2,0:T(8,128)}, u32[]{:S(2)}) copy-start(f32[1,512,12,64]{1,3,2,0:T(8,128)} %multiply_bitcast_fusion.3) | copy-start | bytes 4718596 | tf_op jit(solution)/shard_map/while/body/eval_jaxpr/while
  525.2 3.5 copy-start.9
  532.4 1.9 copy-start.11
  532.4 1.9 copy-start.20
  535.2 1.0 copy-start.18
  536.1 2.0 copy-start
  537.0 2.7 copy-start.26
  538.7 1.4 copy-start.25
  538.8 3.0 copy-start.43
  539.6 7.9 %copy-start.27 = (bf16[1024,12,64]{0,2,1:T(8,128)(2,1)}, bf16[1024,12,64]{0,2,1:T(8,128)(2,1)S(1)}, u32[]{:S(2)}) copy-start(bf16[1024,12,64]{0,2,1:T(8,128)(2,1)S(1)} %fusion.63) | copy-start | bytes 4718596
  548.4 3.7 copy-start.4
  548.4 3.7 copy-start.29
  548.4 3.7 copy-start.31
  548.4 3.7 copy-start.33
  552.1 4.1 copy-start.37
  555.1 109.5 %reduce-scatter.19.cloned.1.call-start = ((), (), s32[]{:S(2)}) async-start(), calls=%async_computation.14 | async-start | bytes 208896
  556.0 179.5 %reduce-scatter.11.cloned.1.call-start = ((), (), s32[]{:S(2)}) async-start(), calls=%async_computation.10 | async-start | bytes 3760128 | tf_op jit(solution)/shard_map/reduce_scatter | solution.py:251
  564.0 3.3 copy-start.15
  564.0 204.7 %all-reduce.4.cloned.1.call-start = ((), (), s32[]{:S(2)}) async-start(), calls=%async_computation.16 | async-start | bytes 1327104 | tf_op jit(solution)/shard_map/psum | solution.py:272
  567.5 5.8 copy-start.12
  567.5 5.8 copy-start.41
  573.3 44.6 %copy-start.22 = (bf16[1024,768]{0,1:T(8,128)(2,1)S(1)}, bf16[1024,768]{0,1:T(8,128)(2,1)}, u32[]{:S(2)}) copy-start(bf16[1024,768]{0,1:T(8,128)(2,1)} %get-tuple-element.533) | copy-start | bytes 4718596
Sparse Core Ops, SparseCore 0:
  10.3 49.9 all-gather.7
  62.5 36.9 all-gather.9
  101.7 52.0 all-gather.11
  155.9 51.7 all-gather.13
  256.4 56.6 reduce-scatter.12
  316.7 74.6 reduce-scatter.14
  395.2 74.7 reduce-scatter.16
  555.2 52.9 reduce-scatter.20
  612.2 52.3 reduce-scatter.18
  668.3 67.1 reduce-scatter.10
  737.9 30.6 all-reduce.3
